TPU v7x, 32 devices: a whole 2x2x4 slice. The times are simulated.
32 devices in a mesh: groups: 2 (over y), tm: 4 (over z), segment: 2 (over x), head: 2 (over core).
Axes of the slice: x: 2, y: 2, z: 4, core: 2. Of those that a mesh axis runs over, the one named last changes fastest.
Arguments:
- hidden_in: bfloat16 [768, 3072], P(('groups', 'tm'), 'head'), parts along dimension 0, may hold values from -6 to 6
- key_cache: bfloat16 [2, 768, 3072], P('segment', ('groups', 'tm'), 'head'), parts along dimension 1, may hold values from -6 to 6
- value_cache: bfloat16 [2, 768, 3072], P('segment', ('groups', 'tm'), 'head'), parts along dimension 1, may hold values from -6 to 6
- query_gain: float32 [2, 128], P('segment'), may hold values from 0.4 to 1.6
- key_gain: float32 [2, 128], P('segment'), may hold values from 0.4 to 1.6
- out_gate: float32 [2, 3072], P('segment', 'head'), may hold values from 0.5 to 2
- span_ids: int32 [768], P('groups'), parts along dimension 0, may hold values from 0 to 2, as said below
Outputs:
- layer_outputs: bfloat16 [2, 768, 3072], P('segment', ('groups', 'tm'), 'head'), parts along dimension 1
There are 2 independent parts, one for each index of `groups`. A program takes and returns all parts, laid end to end along the dimension named above; an argument that names none is the same for every part. Nothing has to cross between parts.
Inputs may be any that keep to these rules, and one draw needn't show every extreme that they name: span_ids never fall and rise by one from span to span; every span but the first and the last holds exactly 192 tokens, and the first and the last together hold 192, each at least one.
All inputs are finite; a program needn't handle non-finite values.
Results may differ from a plain program's by a relative error of at most 0.011.
Values may be sent and summed in bfloat16 or wider, within the bound.
No kernel may reach another device: no remote copies, remote signals or barrier semaphores. Data moves between devices by JAX's collectives and lax.ppermute only.
A program may use at most 64 MiB of HBM per device.

v0:
```python
import math
import jax
import jax.numpy as jnp
from jax import lax
from jax.sharding import PartitionSpec as P

HEAD_DIM = 128


def passed_along(shard, axis, by):
    devices = lax.axis_size(axis)
    pairs = [(i, i + by) for i in range(devices) if 0 <= i + by < devices]
    return lax.ppermute(shard, axis, pairs)


def head_normalize(features, gain_row):
    row_count = features.shape[0]
    shaped = features.astype(jnp.float32).reshape(row_count, -1, HEAD_DIM)
    inverse_rms = lax.rsqrt(jnp.mean(shaped * shaped, axis=-1, keepdims=True) + 1e-06)
    return (shaped * inverse_rms * gain_row).reshape(features.shape).astype(jnp.bfloat16)


def attend_heads(queries, key_rows, value_rows, query_ids, key_ids):
    row_count = queries.shape[0]
    key_count = key_rows.shape[0]
    pair_width = 2 * HEAD_DIM
    group_count = queries.shape[1] // pair_width
    score_scale = 2.0 / math.sqrt(HEAD_DIM)
    allowed = (key_ids[None, :] <= query_ids[:, None]) & (
        key_ids[None, :] >= query_ids[:, None] - 2
    )

    def pair_step(group_index, result):
        column = group_index * pair_width
        query_pair = lax.dynamic_slice_in_dim(queries, column, pair_width, 1).reshape(
            row_count, 2, HEAD_DIM
        )
        key_pair = lax.dynamic_slice_in_dim(key_rows, column, pair_width, 1).reshape(
            key_count, 2, HEAD_DIM
        )
        value_pair = lax.dynamic_slice_in_dim(value_rows, column, pair_width, 1).reshape(
            key_count, 2, HEAD_DIM
        )
        scores = (
            jnp.einsum("rhd,khd->hrk", query_pair, key_pair, preferred_element_type=jnp.float32)
            * score_scale
        )
        weights = jnp.where(allowed[None], jnp.exp(scores), 0.0)
        denominator = jnp.sum(weights, axis=-1)
        mixture = jnp.einsum(
            "hrk,khd->rhd",
            weights.astype(jnp.bfloat16),
            value_pair,
            preferred_element_type=jnp.float32,
        )
        mixture = mixture / jnp.transpose(denominator)[:, :, None]
        return lax.dynamic_update_slice_in_dim(
            result, mixture.reshape(row_count, pair_width), column, 1
        )

    initial = jnp.zeros((row_count, queries.shape[1]), jnp.float32)
    return lax.fori_loop(0, group_count, pair_step, initial)


def body(hidden_in, key_cache, value_cache, query_gain, key_gain, out_gate, span_ids):
    block_rows = hidden_in.shape[0]
    tm_index = lax.axis_index("tm")
    segment_index = lax.axis_index("segment")
    normed_keys = head_normalize(key_cache[0], key_gain[0])
    own_values = value_cache[0]
    first_row = tm_index * block_rows
    all_keys, all_values = (
        lax.all_gather(normed_keys, "tm", axis=0, tiled=True),
        lax.all_gather(own_values, "tm", axis=0, tiled=True),
    )

    def update(row_block):
        queries = head_normalize(row_block, query_gain[0])
        query_ids = lax.dynamic_slice_in_dim(span_ids, first_row, row_block.shape[0], 0)
        mixture = attend_heads(queries, all_keys, all_values, query_ids, span_ids)
        return (row_block.astype(jnp.float32) + out_gate[0] * mixture).astype(jnp.bfloat16)

    segments = lax.axis_size("segment")
    current = hidden_in
    result = hidden_in
    for section in range(segments):
        active = segment_index == section
        produced = lax.cond(active, lambda inputs: update(inputs), lambda inputs: inputs, current)
        result = jnp.where(active, produced, result)
        if section + 1 < segments:
            arrived = passed_along(produced, "segment", 1)
            current = jnp.where(segment_index == section + 1, arrived, current)
    return result[None]


def solution(mesh):
    placed = (
        P(("groups", "tm"), "head"),
        P("segment", ("groups", "tm"), "head"),
        P("segment", ("groups", "tm"), "head"),
        P("segment", None),
        P("segment", None),
        P("segment", "head"),
        P("groups"),
    )
    return jax.shard_map(
        body,
        mesh=mesh,
        in_specs=placed,
        out_specs=P("segment", ("groups", "tm"), "head"),
        check_vma=False,
    )
```

profile of v0, /device:TPU:2, one launch (start us, length us, event | category | flops | bytes accessed | tf_op | source)
XLA Modules:
  0.0 116.2 jit_solution(18251263530535177388)
XLA Ops:
  6.5 1.0 convert_multiply_fusion.4
  7.7 0.3 reduce_sum.53
  8.0 0.1 copy.59
  8.2 0.3 mul.154
  8.5 0.1 copy-done.2
  8.6 0.9 fusion.26
  9.6 0.7 all-gather.6.cloned.1.call-update
  10.4 30.9 %all-gather.4.cloned.1.call-done = bf16[384,1536]{1,0:T(8,128)(2,1)} async-done(((bf16[96,1536]{1,0:T(8,128)(2,1)}), bf16[384,1536]{1,0:T(8,128)(2,1)}) %all-gather.4.cloned.1.call-update) | async-done | bytes 1179664 | tf_op jit(solution)/shard_map/all_gather | solution.py:73
  41.2 31.1 %all-gather.6.cloned.1.call-done = bf16[1,384,1536]{2,1,0:T(8,128)(2,1)} async-done(((bf16[1,96,1536]{2,1,0:T(8,128)(2,1)}), bf16[1,384,1536]{2,1,0:T(8,128)(2,1)}) %all-gather.6.cloned.1.call-update) | async-done | bytes 1179664 | tf_op jit(solution)/shard_map/all_gather | solution.py:74
  72.4 1.3 %collective-permute-start = (bf16[96,1536]{1,0:T(8,128)(2,1)S(1)}, bf16[96,1536]{1,0:T(8,128)(2,1)S(1)}, u32[]{:S(2)}, u32[]{:S(2)}) collective-permute-start(bf16[96,1536]{1,0:T(8,128)(2,1)S(1)} %get-tuple-element.605), channel_id=1, source_target_pairs={{0,2},{1,3},{4,6},{5,7},{8,10},{9,11},{12,14},{13,15},{16,18},{17,... | collective-permute-start | bytes 884744 | tf_op jit(solution)/shard_map/ppermute | solution.py:13
  73.7 20.9 %collective-permute-done = bf16[96,1536]{1,0:T(8,128)(2,1)S(1)} collective-permute-done((bf16[96,1536]{1,0:T(8,128)(2,1)S(1)}, bf16[96,1536]{1,0:T(8,128)(2,1)S(1)}, u32[]{:S(2)}, u32[]{:S(2)}) %collective-permute-start) | collective-permute-done | bytes 294944 | tf_op jit(solution)/shard_map/ppermute | solution.py:13
  94.6 14.0 %conditional.3 = (bf16[96,1536]{1,0:T(8,128)(2,1)S(1)}) conditional(s32[]{:T(128)} %convert_element_type.58, bf16[96,1536]{1,0:T(8,128)(2,1)S(1)} %broadcast_select_fusion, (bf16[96,1536]{1,0:T(8,128)(2,1)S(1)}, f32[1,1536]{1,0:T(1,128)S(1)}, f32[1,128]{1,0:T(1,128)S(1)}, s32[384]{0:T(512)S(1)}, s32[]{:T(128)}, ...), branch_computations={%region_7.8_spmd, %region_8.13_spmd} | conditional | flops 39801896 | bytes 8945361 | solution.py:88
  94.8 0.3 reduce_sum.51
  95.3 0.3 mul.131
  95.6 0.2 fusion.22
  95.9 12.5 %while.27 = (s32[]{:T(128)}, f32[96,1536]{1,0:T(8,128)S(1)}, bf16[384,1536]{1,0:T(8,128)(2,1)}, bf16[96,1536]{1,0:T(8,128)(2,1)S(1)}, bf16[384,1536]{1,0:T(8,128...) while((s32[]{:T(128)}, f32[96,1536]{1,0:T(8,128)S(1)}, ...), condition=%wide.region_12.12_spmd.clone, body=%wide.region_10.11_spmd.clone.sunk | while | flops 38178628 | bytes 2682799 | solution.py:62
  95.9 1.1 constant_dynamic-slice_fusion.6
  97.0 0.2 copy.107
  97.3 0.3 fusion.48
  97.6 0.2 copy.106
  97.7 0.2 fusion.49
  98.0 1.1 constant_dynamic-slice_fusion.6
  99.1 0.2 copy.107
  99.3 0.3 fusion.48
  99.6 0.2 copy.106
  99.8 0.2 fusion.49
  100.1 1.1 constant_dynamic-slice_fusion.6
  101.1 0.2 copy.107
  101.4 0.3 fusion.48
  101.7 0.2 copy.106
  101.9 0.2 fusion.49
  102.2 1.1 constant_dynamic-slice_fusion.6
  103.2 0.2 copy.107
  103.5 0.3 fusion.48
  103.8 0.2 copy.106
  104.0 0.2 fusion.49
  104.3 1.1 constant_dynamic-slice_fusion.6
  105.3 0.2 copy.107
  105.6 0.3 fusion.48
  105.9 0.2 copy.106
  106.1 0.2 fusion.49
  106.3 1.1 constant_dynamic-slice_fusion.6
  107.4 0.2 copy.107
  107.7 0.3 fusion.48
  108.0 0.2 copy.106
  108.1 0.2 fusion.49
  108.4 0.2 fusion.23
  108.6 0.8 select_bitcast_fusion
  (42 shorter events, 1.6 us)
Async XLA Ops:
  6.5 1.6 %copy-start = (f32[1,128]{1,0:T(1,128)S(1)}, f32[1,128]{1,0:T(1,128)}, u32[]{:S(2)}) copy-start(f32[1,128]{1,0:T(1,128)} %param.19) | copy-start | bytes 1540
  6.5 34.7 %all-gather.4.cloned.1.call-start = ((), (), s32[]{:S(2)}) async-start(), calls=%async_computation | async-start | bytes 1474560 | tf_op jit(solution)/shard_map/all_gather | solution.py:73
  7.7 1.0 copy-start.2
  8.5 63.9 %copy-start.1 = (bf16[96,1536]{1,0:T(8,128)(2,1)S(1)}, bf16[96,1536]{1,0:T(8,128)(2,1)}, u32[]{:S(2)}) copy-start(bf16[96,1536]{1,0:T(8,128)(2,1)} %param.15) | copy-start | bytes 884740
  8.5 63.9 %copy-start.3 = (s32[384]{0:T(512)S(1)}, s32[384]{0:T(512)}, u32[]{:S(2)}) copy-start(s32[384]{0:T(512)} %param.21) | copy-start | bytes 4612
  8.5 63.9 %copy-start.4 = (f32[1,1536]{1,0:T(1,128)S(1)}, f32[1,1536]{1,0:T(1,128)}, u32[]{:S(2)}) copy-start(f32[1,1536]{1,0:T(1,128)} %param.20) | copy-start | bytes 18436
  8.5 63.9 %copy-start.5 = (f32[1,128]{1,0:T(1,128)S(1)}, f32[1,128]{1,0:T(1,128)}, u32[]{:S(2)}) copy-start(f32[1,128]{1,0:T(1,128)} %param.18) | copy-start | bytes 1540
  9.6 62.7 %all-gather.6.cloned.1.call-start = ((), (), s32[]{:S(2)}) async-start(), calls=%async_computation.1 | async-start | bytes 1474560 | tf_op jit(solution)/shard_map/all_gather | solution.py:74
  72.4 22.2 %collective-permute-start = (bf16[96,1536]{1,0:T(8,128)(2,1)S(1)}, bf16[96,1536]{1,0:T(8,128)(2,1)S(1)}, u32[]{:S(2)}, u32[]{:S(2)}) collective-permute-start(bf16[96,1536]{1,0:T(8,128)(2,1)S(1)} %get-tuple-element.605), channel_id=1, source_target_pairs={{0,2},{1,3},{4,6},{5,7},{8,10},{9,11},{12,14},{13,15},{16,18},{17,... | collective-permute-start | bytes 884744 | tf_op jit(solution)/shard_map/ppermute | solution.py:13
Sparse Core Ops, SparseCore 0:
  9.7 31.4 all-gather.3
  42.8 29.4 all-gather.5
where the time goes:
time: 116 us
  waiting for transfers between devices  83.5 us (72%)
  between operations  13.5 us (12%)
  local copies, waits for them, and re-layouts  9.74 us (8%)
  other arithmetic  4.47 us (4%)
  matrix products  3.17 us (3%)
  starting transfers between devices  1.34 us (1%)
    all_gather x1, waiting for transfers between devices, body(): lax.all_gather(own_values, 'tm', axis=0, tiled=True)  31.1 us
    all_gather x1, waiting for transfers between devices, body(): lax.all_gather(normed_keys, 'tm', axis=0, tiled=True)  30.9 us
    ppermute x1, waiting for transfers between devices, passed_along(): return lax.ppermute(shard, axis, pairs)  20.9 us
    dynamic_slice x12, local copies, waits for them, and re-layouts, pair_step(): lax.dynamic_slice_in_dim(key_rows, column, pair_width, 1)  7.31 us
  transfers between devices with their start and end apart: 3, of which 3 were waited for; matrix products, arithmetic and copies ran while one was open for 0% of the time, Pallas kernels for 0%

commit v1 on v0

--- a/solution.py
+++ b/solution.py
@@ -70,7 +70,9 @@
     own_values = value_cache[0]
     first_row = tm_index * block_rows
     all_keys, all_values = (
-        lax.all_gather(normed_keys, "tm", axis=0, tiled=True),
+        jnp.concatenate(
+            lax.all_to_all(jnp.stack([normed_keys] * lax.axis_size("tm")), "tm", 0, 0), axis=0
+        ),
         lax.all_gather(own_values, "tm", axis=0, tiled=True),
     )
 

time: 116 us -> 112 us (0.966)
  waiting for transfers between devices: 83.5 us -> 68.8 us
  starting transfers between devices: 1.34 us -> 6.31 us
  other arithmetic: 4.47 us -> 8.28 us
    all_to_all x0 -> x1, waiting for transfers between devices: none -> 45.3 us  [body(): lax.all_to_all(jnp.stack([normed_keys] * lax.axis_size('tm')), 'tm', 0, 0)]
    all_gather x1 -> x0, waiting for transfers between devices: 30.9 us -> none  [body(): lax.all_gather(normed_keys, 'tm', axis=0, tiled=True)]
    all_gather x1, waiting for transfers between devices: 31.1 us -> 1.78 us  [body(): lax.all_gather(own_values, 'tm', axis=0, tiled=True)]
    all_to_all x0 -> x1, starting transfers between devices: none -> 5.01 us  [body(): lax.all_to_all(jnp.stack([normed_keys] * lax.axis_size('tm')), 'tm', 0, 0)]
    and x6, other arithmetic: 0.62 us -> 4.66 us  [attend_heads(): (key_ids[None, :] <= query_ids[:, None]) & (key_ids[None, :] >= query_ids...]
where the time goes in v1:
time: 112 us; the launch traced here: 111 us
  waiting for transfers between devices  68.8 us (61%)
  between operations  13.5 us (12%)
  local copies, waits for them, and re-layouts  10.6 us (9%)
  other arithmetic  8.28 us (7%)
  starting transfers between devices  6.31 us (6%)
  matrix products  3.18 us (3%)
    all_to_all x1, waiting for transfers between devices, body(): lax.all_to_all(jnp.stack([normed_keys] * lax.axis_size('tm')), 'tm', 0, 0)  45.3 us
    ppermute x1, waiting for transfers between devices, passed_along(): return lax.ppermute(shard, axis, pairs)  21 us
    dynamic_slice x12, local copies, waits for them, and re-layouts, pair_step(): lax.dynamic_slice_in_dim(key_rows, column, pair_width, 1)  6.74 us
    all_to_all x1, starting transfers between devices, body(): lax.all_to_all(jnp.stack([normed_keys] * lax.axis_size('tm')), 'tm', 0, 0)  5.01 us
    and x6, other arithmetic, attend_heads(): (key_ids[None, :] <= query_ids[:, None]) & (key_ids[None, :] >= query_ids...  4.66 us
  transfers between devices with their start and end apart: 3, of which 3 were waited for; matrix products, arithmetic and copies ran while one was open for 0% of the time, Pallas kernels for 0%

profile of v1, /device:TPU:2, one launch (start us, length us, event | category | flops | bytes accessed | tf_op | source)
XLA Modules:
  0.0 111.1 jit_solution(617120062675573460)
XLA Ops:
  6.5 1.0 convert_multiply_fusion.5
  7.7 0.3 reduce_sum.53
  8.2 0.3 mul.156
  8.6 0.4 copy-done.2
  9.0 1.1 %stack.10 = bf16[4,96,1536]{2,1,0:T(8,128)(2,1)} broadcast(bf16[96,1536]{1,0:T(8,128)(2,1)S(1)} %fusion.26), dimensions={1,2} | broadcast | bytes 1474560 | tf_op jit(solution)/shard_map/stack | solution.py:74
  10.1 5.0 %all-to-all-start = ((bf16[4,96,1536]{2,1,0:T(8,128)(2,1)}), bf16[4,96,1536]{2,1,0:T(8,128)(2,1)S(1)}, u32[]{:S(2)}, u32[]{:S(2)}) async-start(bf16[4,96,1536]{2,1,0:T(8,128)(2,1)} %stack.10), calls=%async_computation | async-start | bytes 2359296 | tf_op jit(solution)/shard_map/all_to_all | solution.py:74
  15.2 0.7 all-gather.3.cloned.1.call-update
  15.9 45.3 %all-to-all-done = bf16[4,96,1536]{2,1,0:T(8,128)(2,1)S(1)} async-done(((bf16[4,96,1536]{2,1,0:T(8,128)(2,1)}), bf16[4,96,1536]{2,1,0:T(8,128)(2,1)S(1)}, u32[]{:S(2)}, u32[]{:S(2)}) %all-to-all-start) | async-done | bytes 1179680 | tf_op jit(solution)/shard_map/all_to_all | solution.py:74
  61.2 1.8 %all-gather.3.cloned.1.call-done = bf16[1,384,1536]{2,1,0:T(8,128)(2,1)} async-done(((bf16[1,96,1536]{2,1,0:T(8,128)(2,1)}), bf16[1,384,1536]{2,1,0:T(8,128)(2,1)}) %all-gather.3.cloned.1.call-update) | async-done | bytes 1179664 | tf_op jit(solution)/shard_map/all_gather | solution.py:76
  63.1 1.3 %collective-permute-start = (bf16[96,1536]{1,0:T(8,128)(2,1)S(1)}, bf16[96,1536]{1,0:T(8,128)(2,1)S(1)}, u32[]{:S(2)}, u32[]{:S(2)}) collective-permute-start(bf16[96,1536]{1,0:T(8,128)(2,1)S(1)} %get-tuple-element.605), channel_id=1, source_target_pairs={{0,2},{1,3},{4,6},{5,7},{8,10},{9,11},{12,14},{13,15},{16,18},{17,... | collective-permute-start | bytes 884744 | tf_op jit(solution)/shard_map/ppermute | solution.py:13
  64.4 21.0 %collective-permute-done = bf16[96,1536]{1,0:T(8,128)(2,1)S(1)} collective-permute-done((bf16[96,1536]{1,0:T(8,128)(2,1)S(1)}, bf16[96,1536]{1,0:T(8,128)(2,1)S(1)}, u32[]{:S(2)}, u32[]{:S(2)}) %collective-permute-start) | collective-permute-done | bytes 294944 | tf_op jit(solution)/shard_map/ppermute | solution.py:13
  85.4 18.1 %conditional.3 = (bf16[96,1536]{1,0:T(8,128)(2,1)S(1)}) conditional(s32[]{:T(128)} %convert_element_type.55, bf16[96,1536]{1,0:T(8,128)(2,1)S(1)} %broadcast_select_fusion, (bf16[96,1536]{1,0:T(8,128)(2,1)S(1)}, f32[1,1536]{1,0:T(1,128)S(1)}, f32[1,128]{1,0:T(1,128)S(1)}, s32[384]{0:T(512)S(1)}, s32[]{:T(128)}, ...), branch_computations={%region_7.8_spmd, %region_8.13_spmd} | conditional | flops 39801896 | bytes 8945361 | solution.py:90
  85.4 0.7 broadcast_add_fusion.1
  86.3 0.3 reduce_sum.51
  86.8 0.3 mul.133
  87.0 0.2 fusion.22
  87.3 16.0 %while.27 = (s32[]{:T(128)}, f32[96,1536]{1,0:T(8,128)S(1)}, bf16[384,1536]{1,0:T(8,128)(2,1)}, bf16[96,1536]{1,0:T(8,128)(2,1)S(1)}, bf16[384,1536]{1,0:T(8,128...) while((s32[]{:T(128)}, f32[96,1536]{1,0:T(8,128)S(1)}, ...), condition=%wide.region_12.12_spmd.clone, body=%wide.region_10.11_spmd.clone.sunk | while | flops 38178628 | bytes 2682799 | solution.py:62
  87.3 1.0 constant_dynamic-slice_fusion.6
  88.5 0.8 compare_and_fusion.4
  89.3 0.3 fusion.48
  89.6 0.2 copy.114
  89.7 0.2 fusion.49
  90.0 1.0 constant_dynamic-slice_fusion.6
  91.1 0.8 compare_and_fusion.4
  91.9 0.3 fusion.48
  92.2 0.2 copy.114
  92.4 0.2 fusion.49
  92.7 1.0 constant_dynamic-slice_fusion.6
  93.8 0.8 compare_and_fusion.4
  94.6 0.3 fusion.48
  94.9 0.2 copy.114
  95.1 0.2 fusion.49
  95.3 1.0 constant_dynamic-slice_fusion.6
  96.5 0.8 compare_and_fusion.4
  97.2 0.3 fusion.48
  97.5 0.2 copy.114
  97.7 0.2 fusion.49
  98.0 1.0 constant_dynamic-slice_fusion.6
  99.1 0.8 compare_and_fusion.4
  99.9 0.3 fusion.48
  100.2 0.2 copy.114
  100.4 0.2 fusion.49
  100.6 1.0 constant_dynamic-slice_fusion.6
  101.8 0.8 compare_and_fusion.4
  102.6 0.3 fusion.48
  102.9 0.2 copy.114
  103.0 0.2 fusion.49
  103.5 0.8 select_bitcast_fusion
  (43 shorter events, 2.2 us)
Async XLA Ops:
  6.5 2.0 %copy-start = (f32[1,128]{1,0:T(1,128)S(1)}, f32[1,128]{1,0:T(1,128)}, u32[]{:S(2)}) copy-start(f32[1,128]{1,0:T(1,128)} %param.19) | copy-start | bytes 1540
  8.0 1.0 copy-start.2
  10.1 52.9 %copy-start.1 = (bf16[96,1536]{1,0:T(8,128)(2,1)S(1)}, bf16[96,1536]{1,0:T(8,128)(2,1)}, u32[]{:S(2)}) copy-start(bf16[96,1536]{1,0:T(8,128)(2,1)} %param.15) | copy-start | bytes 884740
  10.1 52.9 %copy-start.3 = (s32[384]{0:T(512)S(1)}, s32[384]{0:T(512)}, u32[]{:S(2)}) copy-start(s32[384]{0:T(512)} %param.21) | copy-start | bytes 4612
  10.1 52.9 %copy-start.4 = (f32[1,1536]{1,0:T(1,128)S(1)}, f32[1,1536]{1,0:T(1,128)}, u32[]{:S(2)}) copy-start(f32[1,1536]{1,0:T(1,128)} %param.20) | copy-start | bytes 18436
  10.1 52.9 %copy-start.5 = (f32[1,128]{1,0:T(1,128)S(1)}, f32[1,128]{1,0:T(1,128)}, u32[]{:S(2)}) copy-start(f32[1,128]{1,0:T(1,128)} %param.18) | copy-start | bytes 1540
  10.1 51.1 %all-to-all-start = ((bf16[4,96,1536]{2,1,0:T(8,128)(2,1)}), bf16[4,96,1536]{2,1,0:T(8,128)(2,1)S(1)}, u32[]{:S(2)}, u32[]{:S(2)}) async-start(bf16[4,96,1536]{2,1,0:T(8,128)(2,1)} %stack.10), calls=%async_computation | async-start | bytes 2359296 | tf_op jit(solution)/shard_map/all_to_all | solution.py:74
  15.2 47.8 %all-gather.3.cloned.1.call-start = ((), (), s32[]{:S(2)}) async-start(), calls=%async_computation.1 | async-start | bytes 1474560 | tf_op jit(solution)/shard_map/all_gather | solution.py:76
  63.1 22.3 %collective-permute-start = (bf16[96,1536]{1,0:T(8,128)(2,1)S(1)}, bf16[96,1536]{1,0:T(8,128)(2,1)S(1)}, u32[]{:S(2)}, u32[]{:S(2)}) collective-permute-start(bf16[96,1536]{1,0:T(8,128)(2,1)S(1)} %get-tuple-element.605), channel_id=1, source_target_pairs={{0,2},{1,3},{4,6},{5,7},{8,10},{9,11},{12,14},{13,15},{16,18},{17,... | collective-permute-start | bytes 884744 | tf_op jit(solution)/shard_map/ppermute | solution.py:13
Sparse Core Ops, SparseCore 0:
  17.5 45.4 all-gather.2
